TPU v7x, 512 devices: a whole 4x4x16 slice. The times are simulated.
512 devices in a mesh: expert: 8 (over y, x_lo), dp: 64 (over z, x_hi, core).
Axes of the slice: x: 4 (x_hi: 2, x_lo: 2; x = x_hi * 2 + x_lo), y: 4, z: 16, core: 2. Of those that a mesh axis runs over, the one named last changes fastest.
Arguments:
- x_new: bfloat16 [512, 4096], P('expert', 'dp'), may hold values from -6 to 6
- routes_new: int32 [512, 2], P('expert'), may hold values from 0 to 7, all different within a row; in each aligned block of 64 rows (0 to 63, 64 to 127, ...) at most 32 rows name the same one
- gates_new: float32 [512, 2], P('expert'), may hold values from 0.2 to 1
- w_gate: bfloat16 [8, 4096, 7168], P('expert', None, 'dp'), may hold values from -0.09375 to 0.09375
- w_up: bfloat16 [8, 4096, 7168], P('expert', None, 'dp'), may hold values from -0.09375 to 0.09375
- w_down: bfloat16 [8, 7168, 4096], P('expert', 'dp'), may hold values from -0.1875 to 0.1875
- grad_out: bfloat16 [1024, 4096], P('expert', 'dp'), may hold values from -6 to 6
- routes_old: int32 [1024, 2], P('expert'), may hold values from 0 to 7, all different within a row; in each aligned block of 128 rows (0 to 127, 128 to 255, ...) at most 64 rows name the same one
- gates_old: float32 [1024, 2], P('expert'), may hold values from 0.2 to 1
- pre_gate: bfloat16 [8, 512, 7168], P('expert', None, 'dp'), may hold values from -8 to 8
- pre_up: bfloat16 [8, 512, 7168], P('expert', None, 'dp'), may hold values from -6 to 6
Outputs:
- mixed: bfloat16 [512, 4096], P('expert', 'dp')
- grad_down: bfloat16 [8, 7168, 4096], P('expert', 'dp')
- grad_gate: bfloat16 [8, 512, 7168], P('expert', None, 'dp')
- grad_up: bfloat16 [8, 512, 7168], P('expert', None, 'dp')
Inputs may be any that keep to these rules, and one draw needn't show every extreme that they name: `routes_new`: in each group of 64 tokens each expert is named by at most 32 tokens, and by exactly 32 tokens in some group; the two experts of a token differ. `routes_old`: in each group of 128 tokens each expert is named by at most 64 tokens, and by exactly 64 tokens in some group; the two experts of a token differ.
All inputs are finite; a program needn't handle non-finite values.
Results may differ from a plain program's by a relative error of at most 0.0078.
Values may be sent and summed in bfloat16 or wider, within the bound.
No kernel may reach another device: no remote copies, remote signals or barrier semaphores. Data moves between devices by JAX's collectives and lax.ppermute only.
A program may use at most 64 MiB of HBM per device.

v0:
```python
import jax
import jax.numpy as jnp
from jax import lax
from jax.sharding import Mesh
from jax.sharding import PartitionSpec as P

CAP_B = 32
CAP_A = 64
EXPERT = ("expert_0", "expert_1")
DP = ("dp_0", "dp_1", "dp_2")


def split_up(array, dim, size):
    before, after = (array.shape[:dim], array.shape[dim + 1 :])
    return jnp.moveaxis(array.reshape(*before, size, -1, *after), dim, 0)


def in_order(parts, dim):
    parts = jnp.moveaxis(parts, 0, dim)
    shape = parts.shape
    return parts.reshape(*shape[:dim], shape[dim] * shape[dim + 1], *shape[dim + 2 :])


def turned_blocks(parts, axes, turns):
    shape = [lax.axis_size(a) for a in axes]
    parts = parts.reshape(*shape, *parts.shape[1:])
    for k in turns:
        parts = lax.all_to_all(parts, axes[k], split_axis=k, concat_axis=k, tiled=True)
    return parts.reshape(-1, *parts.shape[len(axes) :])


def stepwise_exchange(array, axes, turns, split_dim, concat_dim):
    parts = split_up(array, split_dim, lax.axis_size(axes))
    return in_order(turned_blocks(parts, axes, turns), concat_dim)


def sum_at_owner(array, axis, dim):
    parts = split_up(array, dim, lax.axis_size(axis))
    arrived = lax.all_to_all(parts, axis, split_axis=0, concat_axis=0, tiled=True)
    return arrived.astype(jnp.float32).sum(axis=0)


def gather_in_order(array, axes, turns):
    parts = array[None]
    for k in turns:
        parts = lax.all_gather(parts, axes[k], axis=0, tiled=True)
    current = [lax.axis_size(axes[k]) for k in reversed(turns)]
    parts = parts.reshape(*current, *array.shape)
    turned = sorted(range(len(turns)), key=lambda place: turns[len(turns) - 1 - place])
    return parts.transpose(*turned, *range(len(turns), parts.ndim)).reshape(-1, *array.shape)


def gather_axes(array, axes, turns, dim):
    return in_order(gather_in_order(array, axes, turns), dim)


def slot_table(routes, capacity, experts):
    pairs = routes.reshape(-1)
    onehot = (pairs[:, None] == jnp.arange(experts, dtype=jnp.int32)[None, :]).astype(jnp.int32)
    before = jnp.cumsum(onehot, axis=0) - onehot
    slot = jnp.sum(before * onehot, axis=1)
    column = pairs * capacity + slot
    table = (jnp.arange(experts * capacity, dtype=jnp.int32)[:, None] == column[None, :]).astype(
        jnp.float32
    )
    return table.reshape(experts * capacity, routes.shape[0], 2)


def per_device(
    x_new,
    routes_new,
    gates_new,
    w_gate,
    w_up,
    w_down,
    grad_out,
    routes_old,
    gates_old,
    pre_gate,
    pre_up,
):
    experts = lax.axis_size(EXPERT)
    slice_width = x_new.shape[1]
    gate_weight = w_gate[0]
    up_weight = w_up[0]
    down_weight = w_down[0]
    rows_new = experts * CAP_B
    rows_old = experts * CAP_A
    table_new = slot_table(routes_new, CAP_B, experts)
    picks = jnp.sum(table_new, axis=2).astype(jnp.bfloat16)
    outgoing = jnp.dot(picks, x_new, preferred_element_type=jnp.float32).astype(jnp.bfloat16)
    arrived = stepwise_exchange(outgoing.reshape(experts, CAP_B, slice_width), EXPERT, (0, 1), 0, 0)
    arrived = arrived.reshape(rows_new, slice_width)
    piece = lax.all_gather(arrived, DP, axis=1, tiled=True)
    gate_pre = jnp.dot(piece, gate_weight, preferred_element_type=jnp.float32)
    up_pre = jnp.dot(piece, up_weight, preferred_element_type=jnp.float32)
    hidden = (jax.nn.silu(gate_pre) * up_pre).astype(jnp.bfloat16)
    partial_value = jnp.dot(hidden, down_weight, preferred_element_type=jnp.float32)
    result = sum_at_owner(partial_value.astype(jnp.bfloat16), DP, 1).astype(jnp.bfloat16)
    returned = lax.all_to_all(
        result.reshape(experts, CAP_B, slice_width), EXPERT, split_axis=0, concat_axis=0, tiled=True
    )
    returned = returned.reshape(rows_new, slice_width)
    weights_new = jnp.sum(table_new * gates_new[None, :, :], axis=2)
    mixed = jnp.dot(
        weights_new.T, returned.astype(jnp.float32), precision=lax.Precision.HIGHEST
    ).astype(jnp.bfloat16)
    table_old = slot_table(routes_old, CAP_A, experts)
    weights_old = jnp.sum(table_old * gates_old[None, :, :], axis=2)
    cotangent = jnp.dot(
        weights_old, grad_out.astype(jnp.float32), precision=lax.Precision.HIGHEST
    ).astype(jnp.bfloat16)
    landed = stepwise_exchange(cotangent.reshape(experts, CAP_A, slice_width), EXPERT, (0, 1), 0, 0)
    landed = landed.reshape(rows_old, slice_width)
    saved_gate = pre_gate[0].astype(jnp.float32)
    saved_up = pre_up[0].astype(jnp.float32)
    sigma = jax.nn.sigmoid(saved_gate)
    active = saved_gate * sigma
    hidden_old = (active * saved_up).astype(jnp.bfloat16)
    piece = gather_axes(landed, DP, (1, 0, 2), 1)
    grad_hidden = lax.dot_general(
        piece, down_weight, (((1,), (1,)), ((), ())), preferred_element_type=jnp.float32
    )
    block = lax.dot_general(
        hidden_old, piece, (((0,), (0,)), ((), ())), preferred_element_type=jnp.float32
    )
    weight_grad = block
    grad_hidden, weight_grad = (grad_hidden, weight_grad)
    gate_grad = (grad_hidden * saved_up * sigma * (1.0 + saved_gate * (1.0 - sigma))).astype(
        jnp.bfloat16
    )
    up_grad = (grad_hidden * active).astype(jnp.bfloat16)
    return (mixed, weight_grad.astype(jnp.bfloat16)[None], gate_grad[None], up_grad[None])


def solution(mesh):
    torus = Mesh(
        mesh.devices.reshape(4, 2, 16, 2, 2), ("expert_0", "expert_1", "dp_0", "dp_1", "dp_2")
    )
    placed = (
        P(EXPERT, DP),
        P(EXPERT, None),
        P(EXPERT, None),
        P(EXPERT, None, DP),
        P(EXPERT, None, DP),
        P(EXPERT, DP, None),
        P(EXPERT, DP),
        P(EXPERT, None),
        P(EXPERT, None),
        P(EXPERT, None, DP),
        P(EXPERT, None, DP),
    )
    return jax.shard_map(
        per_device,
        mesh=torus,
        in_specs=placed,
        out_specs=(P(EXPERT, DP), P(EXPERT, DP, None), P(EXPERT, None, DP), P(EXPERT, None, DP)),
        check_vma=False,
    )
```

profile of v0, /device:TPU:1, one launch (start us, length us, event | category | flops | bytes accessed | tf_op | source)
XLA Modules:
  0.0 352.6 jit_solution(8660613464620570664)
XLA Ops:
  7.2 0.8 copy.102
  8.1 0.1 eq.69
  8.3 0.2 reduce_window_sum.26
  8.5 0.2 select_reduce_fusion.2
  8.7 0.1 reduce_sum.62
  8.9 0.7 multiply_add_fusion.1
  9.6 0.8 convert_reduce_fusion
  10.4 0.9 convolution_convert_fusion.3
  11.4 0.1 reshape.97
  11.5 9.1 %all_to_all.30 = bf16[4,2,2048]{2,1,0:T(2,128)(2,1)S(1)} all-to-all(bf16[4,2,2048]{2,1,0:T(2,128)(2,1)S(1)} %reshape.97), channel_id=1, replica_groups=mesh['expert_0'=4,'expert_1'=2,'dp_0'=16,'dp_1'=2,'dp_2'=2] {'expert_0'}, dimensions={0} | all-to-all | bytes 65536 | tf_op jit(solution)/shard_map/all_to_all | solution.py:28
  20.8 0.1 reshape.99
  20.9 5.2 %all_to_all.31 = bf16[2,2,4096]{2,1,0:T(2,128)(2,1)S(1)} all-to-all(bf16[2,2,4096]{2,1,0:T(2,128)(2,1)S(1)} %reshape.99), channel_id=1, replica_groups=mesh['expert_0'=4,'expert_1'=2,'dp_0'=16,'dp_1'=2,'dp_2'=2] {'expert_1'}, dimensions={0} | all-to-all | bytes 65536 | tf_op jit(solution)/shard_map/all_to_all | solution.py:28
  26.2 0.7 copy.108
  27.0 0.8 copy.111
  27.7 0.1 eq.80
  27.9 0.1 eq.76
  28.0 0.6 reduce-window.6
  28.6 0.2 slice_reduce_fusion
  29.0 0.1 reduce_sum.67
  29.2 0.7 multiply_add_fusion
  29.9 0.8 select_reduce_fusion
  30.7 0.3 convolution_convert_fusion.2
  31.0 0.1 reshape_reshape_reshape.11
  31.2 0.2 reshape.103
  31.4 6.8 %all_to_all.32 = bf16[4,2,4096]{2,1,0:T(2,128)(2,1)S(1)} all-to-all(bf16[4,2,4096]{2,1,0:T(2,128)(2,1)S(1)} %reshape.103), channel_id=1, replica_groups=mesh['expert_0'=4,'expert_1'=2,'dp_0'=16,'dp_1'=2,'dp_2'=2] {'expert_0'}, dimensions={0} | all-to-all | bytes 131072 | tf_op jit(solution)/shard_map/all_to_all | solution.py:28
  38.2 0.1 reshape.104
  38.5 0.2 reshape.105
  38.6 5.4 %all_to_all.33 = bf16[2,2,8192]{2,1,0:T(2,128)(2,1)S(1)} all-to-all(bf16[2,2,8192]{2,1,0:T(2,128)(2,1)S(1)} %reshape.105), channel_id=1, replica_groups=mesh['expert_0'=4,'expert_1'=2,'dp_0'=16,'dp_1'=2,'dp_2'=2] {'expert_1'}, dimensions={0} | all-to-all | bytes 131072 | tf_op jit(solution)/shard_map/all_to_all | solution.py:28
  44.0 0.1 reshape.106
  44.1 0.1 copy.116
  44.3 0.1 broadcast_in_dim_reshape_reshape_reshape.3
  44.4 5.7 %all_gather.13 = bf16[2,512,64]{1,2,0:T(8,128)(2,1)} all-gather(bf16[1,512,64]{1,2,0:T(8,128)(2,1)S(1)} %broadcast_in_dim_reshape_reshape_reshape.3), channel_id=1, replica_groups=mesh['expert_0'=4,'expert_1'=2,'dp_0'=16,'dp_1'=2,'dp_2'=2] {'dp_1'}, dimensions={0}, use_global_device_ids=true | all-gather | bytes 196608 | tf_op jit(solution)/shard_map/all_gather | solution.py:46
  50.2 126.3 %all-gather.4.cloned.1.call-done = bf16[256,4096]{0,1:T(8,128)(2,1)} async-done(((bf16[256,64]{0,1:T(8,128)(2,1)}), bf16[256,4096]{0,1:T(8,128)(2,1)}) %all-gather.4.cloned.1.call-update) | async-done | bytes 2097168 | tf_op jit(solution)/shard_map/all_gather | solution.py:94
  176.4 2.5 fusion.7
  178.9 4.2 %convolution_convert_fusion = bf16[256,4096]{1,0:T(8,128)(2,1)} fusion(bf16[256,4096]{0,1:T(8,128)(2,1)S(1)} %copy-done.2, bf16[1,112,4096]{2,1,0:T(8,128)(2,1)S(1)} %copy-done, bf16[1,4096,112]{1,2,0:T(8,128)(2,1)} %param.15, f32[256,112]{0,1:T(8,128)S(1)} %fusion.7), kind=kOutput, calls=%fused_computation | convolution fusion | flops 470982656 | bytes 6144000 | tf_op jit(solution)/shard_map/dot_general | solution.py:98
  183.1 4.1 %copy.109 = bf16[256,4096]{0,1:T(8,128)(2,1)} copy(bf16[256,4096]{1,0:T(8,128)(2,1)} %convolution_convert_fusion) | data formatting | bytes 4194304 | tf_op jit(solution)/shard_map/convert_element_type | solution.py:99
  187.2 7.9 %all-to-all-start.2 = ((bf16[64,256,64]{1,2,0:T(8,128)(2,1)}), bf16[64,256,64]{1,2,0:T(8,128)(2,1)S(1)}, u32[]{:S(2)}, u32[]{:S(2)}) async-start(bf16[64,256,64]{1,2,0:T(8,128)(2,1)} %bitcast.121), calls=%async_computation.2 | async-start | bytes 4194304 | tf_op jit(solution)/shard_map/all_to_all | solution.py:39
  195.1 102.4 %all-gather.6.cloned.1.call-done = bf16[32,512,64]{1,2,0:T(8,128)(2,1)} async-done(((bf16[2,512,64]{1,2,0:T(8,128)(2,1)}), bf16[32,512,64]{1,2,0:T(8,128)(2,1)}) %all-gather.6.cloned.1.call-update) | async-done | bytes 2097168 | tf_op jit(solution)/shard_map/all_gather | solution.py:46
  297.6 31.2 %all-gather.8.cloned.1.call-done = bf16[64,512,64]{1,2,0:T(8,128)(2,1)} async-done(((bf16[32,512,64]{1,2,0:T(8,128)(2,1)}), bf16[64,512,64]{1,2,0:T(8,128)(2,1)}) %all-gather.8.cloned.1.call-update) | async-done | bytes 4194320 | tf_op jit(solution)/shard_map/all_gather | solution.py:46
  328.8 2.7 copy.117
  331.6 1.9 copy-done.1
  333.5 1.5 fusion.33
  335.0 0.3 reduce_sum.65
  335.4 0.7 reshape.101
  336.1 3.9 %all-to-all-start.3 = ((bf16[8,2,1024]{2,1,0:T(2,128)(2,1)}), bf16[8,2,1024]{2,1,0:T(2,128)(2,1)S(1)}, u32[]{:S(2)}, u32[]{:S(2)}) async-start(bf16[8,2,1024]{2,1,0:T(2,128)(2,1)} %reshape.101), calls=%async_computation.3 | async-start | bytes 65536 | tf_op jit(solution)/shard_map/all_to_all | solution.py:100
  340.0 4.5 %fusion = bf16[1,112,4096]{2,1,0:T(8,128)(2,1)} fusion(bf16[512,4096]{0,1:T(8,128)(2,1)} %bitcast.120, bf16[1,512,112]{1,2,0:T(8,128)(2,1)S(1)} %copy-done.3, bf16[1,512,112]{1,2,0:T(8,128)(2,1)S(1)} %copy-done.4), kind=kOutput, calls=%fused_computation.2 | convolution fusion | flops 470679552 | bytes 5341184 | tf_op jit(solution)/shard_map/dot_general | solution.py:124
  344.6 0.6 all-to-all-done.3
  345.2 0.8 convolution_convert_fusion.4
  (34 shorter events, 1.3 us)
Async XLA Ops:
  7.2 171.7 %copy-start = (bf16[1,112,4096]{2,1,0:T(8,128)(2,1)S(1)}, bf16[1,112,4096]{2,1,0:T(8,128)(2,1)}, u32[]{:S(2)}) copy-start(bf16[1,112,4096]{2,1,0:T(8,128)(2,1)} %param.16) | copy-start | bytes 2752516
  7.2 23.5 %copy-start.5 = (bf16[128,64]{0,1:T(8,128)(2,1)S(1)}, bf16[128,64]{0,1:T(8,128)(2,1)}, u32[]{:S(2)}) copy-start(bf16[128,64]{0,1:T(8,128)(2,1)} %param.17) | copy-start | bytes 49156
  7.2 169.2 %all-gather.4.cloned.1.call-start = ((), (), s32[]{:S(2)}) async-start(), calls=%async_computation.6 | async-start | bytes 2129920 | tf_op jit(solution)/shard_map/all_gather | solution.py:94
  26.9 270.7 %all-gather.6.cloned.1.call-start = ((), (), s32[]{:S(2)}) async-start(), calls=%async_computation.7 | async-start | bytes 2228224 | tf_op jit(solution)/shard_map/all_gather | solution.py:46
  176.4 2.5 copy-start.2
  187.2 147.8 %all-to-all-start.2 = ((bf16[64,256,64]{1,2,0:T(8,128)(2,1)}), bf16[64,256,64]{1,2,0:T(8,128)(2,1)S(1)}, u32[]{:S(2)}, u32[]{:S(2)}) async-start(bf16[64,256,64]{1,2,0:T(8,128)(2,1)} %bitcast.121), calls=%async_computation.2 | async-start | bytes 4194304 | tf_op jit(solution)/shard_map/all_to_all | solution.py:39
  195.1 133.7 %all-gather.8.cloned.1.call-start = ((), (), s32[]{:S(2)}) async-start(), calls=%async_computation.8 | async-start | bytes 6291456 | tf_op jit(solution)/shard_map/all_gather | solution.py:46
  328.8 4.7 %copy-start.3 = (bf16[1,512,112]{1,2,0:T(8,128)(2,1)S(1)}, bf16[1,512,112]{1,2,0:T(8,128)(2,1)}, u32[]{:S(2)}) copy-start(bf16[1,512,112]{1,2,0:T(8,128)(2,1)} %param.21) | copy-start | bytes 344068
  328.8 4.7 %copy-start.4 = (bf16[1,512,112]{1,2,0:T(8,128)(2,1)S(1)}, bf16[1,512,112]{1,2,0:T(8,128)(2,1)}, u32[]{:S(2)}) copy-start(bf16[1,512,112]{1,2,0:T(8,128)(2,1)} %param.20) | copy-start | bytes 344068
  331.6 1.9 copy-start.1
  336.1 9.0 %all-to-all-start.3 = ((bf16[8,2,1024]{2,1,0:T(2,128)(2,1)}), bf16[8,2,1024]{2,1,0:T(2,128)(2,1)S(1)}, u32[]{:S(2)}, u32[]{:S(2)}) async-start(bf16[8,2,1024]{2,1,0:T(2,128)(2,1)} %reshape.101), calls=%async_computation.3 | async-start | bytes 65536 | tf_op jit(solution)/shard_map/all_to_all | solution.py:100
Sparse Core Ops, SparseCore 0:
  27.0 149.3 all-gather.3
  178.5 119.0 all-gather.5
  299.7 29.1 all-gather.7
where the time goes:
time: 353 us
  waiting for transfers between devices  261 us (74%)
  blocking collectives  32.2 us (9%)
  local copies, waits for them, and re-layouts  14.9 us (4%)
  matrix products  14.6 us (4%)
  between operations  14 us (4%)
  starting transfers between devices  11.9 us (3%)
  other arithmetic  4.41 us (1%)
    all_gather x2, waiting for transfers between devices, gather_in_order(): parts = lax.all_gather(parts, axes[k], axis=0, tiled=True)  134 us
    all_gather x1, waiting for transfers between devices, per_device(): piece = lax.all_gather(arrived, DP, axis=1, tiled=True)  126 us
    all_to_all x4, blocking collectives, turned_blocks(): lax.all_to_all(parts, axes[k], split_axis=k, concat_axis=k, tiled=True)  26.5 us
    all_to_all x1, starting transfers between devices, sum_at_owner(): lax.all_to_all(parts, axis, split_axis=0, concat_axis=0, tiled=True)  7.87 us
  transfers between devices with their start and end apart: 5, of which 4 were waited for; matrix products, arithmetic and copies ran while one was open for 7% of the time, Pallas kernels for 0%

commit v1 on v0

--- a/solution.py
+++ b/solution.py
@@ -91,7 +91,10 @@
     outgoing = jnp.dot(picks, x_new, preferred_element_type=jnp.float32).astype(jnp.bfloat16)
     arrived = stepwise_exchange(outgoing.reshape(experts, CAP_B, slice_width), EXPERT, (0, 1), 0, 0)
     arrived = arrived.reshape(rows_new, slice_width)
-    piece = lax.all_gather(arrived, DP, axis=1, tiled=True)
+    count = lax.axis_size(DP)
+    pieces = jnp.stack([arrived for _ in range(count)])
+    pieces = lax.all_to_all(pieces, DP, split_axis=0, concat_axis=0)
+    piece = jnp.concatenate(pieces, axis=1)
     gate_pre = jnp.dot(piece, gate_weight, preferred_element_type=jnp.float32)
     up_pre = jnp.dot(piece, up_weight, preferred_element_type=jnp.float32)
     hidden = (jax.nn.silu(gate_pre) * up_pre).astype(jnp.bfloat16)

time: 353 us -> 321 us (0.909); the launches traced: 353 us -> 317 us
  waiting for transfers between devices: 261 us -> 209 us
  starting transfers between devices: 11.9 us -> 49.7 us
  blocking collectives: 32.2 us -> 6.25 us
    all_gather x1 -> x0, waiting for transfers between devices: 126 us -> none  [per_device(): piece = lax.all_gather(arrived, DP, axis=1, tiled=True)]
    all_to_all x0 -> x5, waiting for transfers between devices: none -> 117 us  [the longest x1 108 us: per_device(): pieces = lax.all_to_all(pieces, DP, split_axis=0, concat_axis=0)]
    all_gather x2, waiting for transfers between devices: 134 us -> 26 us  [gather_in_order(): parts = lax.all_gather(parts, axes[k], axis=0, tiled=True)]
    all_to_all x1, waiting for transfers between devices: 0.01 us -> 65.5 us  [sum_at_owner(): lax.all_to_all(parts, axis, split_axis=0, concat_axis=0, tiled=True)]
    all_to_all x0 -> x5, starting transfers between devices: none -> 38.6 us  [the longest x1 22.8 us: per_device(): pieces = lax.all_to_all(pieces, DP, split_axis=0, concat_axis=0)]
    all_to_all x4 -> x0, blocking collectives: 26.5 us -> none  [turned_blocks(): lax.all_to_all(parts, axes[k], split_axis=k, concat_axis=k, tiled=True)]
    unnamed x25 -> x21, local copies, waits for them, and re-layouts: 5.5 us -> 7.98 us
  transfers between devices with their start and end apart: 5 -> 9, of which waited for: 4 -> 7; matrix products, arithmetic and copies ran while one was open for 7% -> 8% of each run, Pallas kernels for 0% -> 0%
where the time goes in v1:
time: 321 us; the launch traced here: 317 us
  waiting for transfers between devices  209 us (65%)
  starting transfers between devices  49.7 us (15%)
  local copies, waits for them, and re-layouts  18.4 us (6%)
  matrix products  14.5 us (5%)
  between operations  14.3 us (4%)
  blocking collectives  6.25 us (2%)
  other arithmetic  4.41 us (1%)
    all_to_all x1, waiting for transfers between devices, per_device(): pieces = lax.all_to_all(pieces, DP, split_axis=0, concat_axis=0)  108 us
    all_to_all x1, waiting for transfers between devices, sum_at_owner(): lax.all_to_all(parts, axis, split_axis=0, concat_axis=0, tiled=True)  65.5 us
    all_gather x2, waiting for transfers between devices, gather_in_order(): parts = lax.all_gather(parts, axes[k], axis=0, tiled=True)  26 us
    all_to_all x1, starting transfers between devices, per_device(): pieces = lax.all_to_all(pieces, DP, split_axis=0, concat_axis=0)  22.8 us
    all_to_all x4, starting transfers between devices, turned_blocks(): lax.all_to_all(parts, axes[k], split_axis=k, concat_axis=k, tiled=True)  15.8 us
    all_to_all x4, waiting for transfers between devices, turned_blocks(): lax.all_to_all(parts, axes[k], split_axis=k, concat_axis=k, tiled=True)  8.37 us
    unnamed x21, local copies, waits for them, and re-layouts  7.98 us
    all_to_all x1, starting transfers between devices, sum_at_owner(): lax.all_to_all(parts, axis, split_axis=0, concat_axis=0, tiled=True)  7.67 us
  transfers between devices with their start and end apart: 9, of which 7 were waited for; matrix products, arithmetic and copies ran while one was open for 8% of the time, Pallas kernels for 0%

profile of v1, /device:TPU:1, one launch (start us, length us, event | category | flops | bytes accessed | tf_op | source)
XLA Modules:
  0.0 316.8 jit_solution(5156740645625930066)
XLA Ops:
  7.2 0.8 copy.105
  8.3 0.2 reduce_window_sum.26
  8.4 0.2 select_reduce_fusion.2
  8.6 0.1 reduce_sum.62
  8.8 0.7 multiply_add_fusion.1
  9.5 0.8 convert_reduce_fusion
  10.3 0.9 convolution_convert_fusion.3
  11.4 0.7 reshape.107
  12.1 5.0 %all-to-all-start = ((bf16[4,2,2048]{2,1,0:T(2,128)(2,1)}), bf16[4,2,2048]{2,1,0:T(2,128)(2,1)S(1)}, u32[]{:S(2)}, u32[]{:S(2)}) async-start(bf16[4,2,2048]{2,1,0:T(2,128)(2,1)} %reshape.107), calls=%async_computation | async-start | bytes 65536 | tf_op jit(solution)/shard_map/all_to_all | solution.py:28
  17.1 0.8 copy.114
  18.2 0.6 reduce-window.6
  18.8 0.2 slice_reduce_fusion
  19.1 0.1 reduce_sum.67
  19.3 0.7 multiply_add_fusion
  20.0 0.8 select_reduce_fusion
  20.8 1.0 convolution_convert_fusion.2
  22.1 0.8 reshape.113
  22.9 4.2 %all-to-all-start.5 = ((bf16[4,2,4096]{2,1,0:T(2,128)(2,1)}), bf16[4,2,4096]{2,1,0:T(2,128)(2,1)S(1)}, u32[]{:S(2)}, u32[]{:S(2)}) async-start(bf16[4,2,4096]{2,1,0:T(2,128)(2,1)} %reshape.113), calls=%async_computation.5 | async-start | bytes 131072 | tf_op jit(solution)/shard_map/all_to_all | solution.py:28
  27.2 0.7 reshape.109
  28.0 3.6 %all-to-all-done.5 = bf16[4,2,4096]{2,1,0:T(2,128)(2,1)S(1)} async-done(((bf16[4,2,4096]{2,1,0:T(2,128)(2,1)}), bf16[4,2,4096]{2,1,0:T(2,128)(2,1)S(1)}, u32[]{:S(2)}, u32[]{:S(2)}) %all-to-all-start.5) | async-done | bytes 65568 | tf_op jit(solution)/shard_map/all_to_all | solution.py:28
  31.6 3.3 %all-to-all-start.1 = ((bf16[2,2,4096]{2,1,0:T(2,128)(2,1)}), bf16[2,2,4096]{2,1,0:T(2,128)(2,1)S(1)}, u32[]{:S(2)}, u32[]{:S(2)}) async-start(bf16[2,2,4096]{2,1,0:T(2,128)(2,1)} %reshape.109), calls=%async_computation.1 | async-start | bytes 65536 | tf_op jit(solution)/shard_map/all_to_all | solution.py:28
  34.8 0.1 reshape.114
  35.1 0.8 reshape.115
  35.9 2.0 all-to-all-done.1
  37.9 3.3 %all-to-all-start.6 = ((bf16[2,2,8192]{2,1,0:T(2,128)(2,1)}), bf16[2,2,8192]{2,1,0:T(2,128)(2,1)S(1)}, u32[]{:S(2)}, u32[]{:S(2)}) async-start(bf16[2,2,8192]{2,1,0:T(2,128)(2,1)} %reshape.115), calls=%async_computation.6 | async-start | bytes 131072 | tf_op jit(solution)/shard_map/all_to_all | solution.py:28
  41.4 2.7 all-to-all-done.6
  44.2 1.6 stack.3
  45.8 22.8 %all-to-all-start.2 = ((bf16[64,256,64]{1,2,0:T(8,128)(2,1)}), bf16[64,256,64]{1,2,0:T(8,128)(2,1)S(1)}, u32[]{:S(2)}, u32[]{:S(2)}) async-start(bf16[64,256,64]{1,2,0:T(8,128)(2,1)} %stack.3), calls=%async_computation.2 | async-start | bytes 4194304 | tf_op jit(solution)/shard_map/all_to_all | solution.py:96
  68.6 0.1 reshape.116
  68.9 0.1 broadcast_in_dim_reshape_reshape_reshape.3
  69.0 6.3 %all_gather.9 = bf16[2,512,64]{1,2,0:T(8,128)(2,1)} all-gather(bf16[1,512,64]{1,2,0:T(8,128)(2,1)S(1)} %broadcast_in_dim_reshape_reshape_reshape.3), channel_id=1, replica_groups=mesh['expert_0'=4,'expert_1'=2,'dp_0'=16,'dp_1'=2,'dp_2'=2] {'dp_1'}, dimensions={0}, use_global_device_ids=true | all-gather | bytes 196608 | tf_op jit(solution)/shard_map/all_gather | solution.py:46
  75.3 108.2 %all-to-all-done.2 = bf16[64,256,64]{1,2,0:T(8,128)(2,1)S(1)} async-done(((bf16[64,256,64]{1,2,0:T(8,128)(2,1)}), bf16[64,256,64]{1,2,0:T(8,128)(2,1)S(1)}, u32[]{:S(2)}, u32[]{:S(2)}) %all-to-all-start.2) | async-done | bytes 2097184 | tf_op jit(solution)/shard_map/all_to_all | solution.py:96
  183.6 1.6 fusion.7
  185.2 4.2 %convolution_convert_fusion = bf16[256,4096]{1,0:T(8,128)(2,1)} fusion(bf16[256,4096]{0,1:T(8,128)(2,1)S(1)} %bitcast.123, bf16[1,112,4096]{2,1,0:T(8,128)(2,1)S(1)} %copy-done, bf16[1,4096,112]{1,2,0:T(8,128)(2,1)} %param.15, f32[256,112]{0,1:T(8,128)S(1)} %fusion.7), kind=kOutput, calls=%fused_computation | convolution fusion | flops 470982656 | bytes 6144000 | tf_op jit(solution)/shard_map/dot_general | solution.py:101
  189.4 4.1 %copy.112 = bf16[256,4096]{0,1:T(8,128)(2,1)} copy(bf16[256,4096]{1,0:T(8,128)(2,1)} %convolution_convert_fusion) | data formatting | bytes 4194304 | tf_op jit(solution)/shard_map/convert_element_type | solution.py:102
  193.5 7.7 %all-to-all-start.3 = ((bf16[64,256,64]{1,2,0:T(8,128)(2,1)}), bf16[64,256,64]{1,2,0:T(8,128)(2,1)S(1)}, u32[]{:S(2)}, u32[]{:S(2)}) async-start(bf16[64,256,64]{1,2,0:T(8,128)(2,1)} %bitcast.126), calls=%async_computation.3 | async-start | bytes 4194304 | tf_op jit(solution)/shard_map/all_to_all | solution.py:39
  201.2 0.7 all-gather.5.cloned.1.call-update
  201.9 26.0 %all-gather.5.cloned.1.call-done = bf16[64,512,64]{1,2,0:T(8,128)(2,1)} async-done(((bf16[32,512,64]{1,2,0:T(8,128)(2,1)}), bf16[64,512,64]{1,2,0:T(8,128)(2,1)}) %all-gather.5.cloned.1.call-update) | async-done | bytes 4194320 | tf_op jit(solution)/shard_map/all_gather | solution.py:46
  227.9 2.7 copy.120
  230.6 1.9 copy-done.1
  232.6 1.5 fusion.33
  234.0 65.5 %all-to-all-done.3 = bf16[64,256,64]{1,2,0:T(8,128)(2,1)S(1)} async-done(((bf16[64,256,64]{1,2,0:T(8,128)(2,1)}), bf16[64,256,64]{1,2,0:T(8,128)(2,1)S(1)}, u32[]{:S(2)}, u32[]{:S(2)}) %all-to-all-start.3) | async-done | bytes 2097184 | tf_op jit(solution)/shard_map/all_to_all | solution.py:39
  299.5 0.3 reduce_sum.65
  299.9 0.7 reshape.111
  300.7 3.3 %all-to-all-start.4 = ((bf16[8,2,1024]{2,1,0:T(2,128)(2,1)}), bf16[8,2,1024]{2,1,0:T(2,128)(2,1)S(1)}, u32[]{:S(2)}, u32[]{:S(2)}) async-start(bf16[8,2,1024]{2,1,0:T(2,128)(2,1)} %reshape.111), calls=%async_computation.4 | async-start | bytes 65536 | tf_op jit(solution)/shard_map/all_to_all | solution.py:103
  304.0 4.5 %fusion = bf16[1,112,4096]{2,1,0:T(8,128)(2,1)} fusion(bf16[512,4096]{0,1:T(8,128)(2,1)} %bitcast.125, bf16[1,512,112]{1,2,0:T(8,128)(2,1)S(1)} %copy-done.2, bf16[1,512,112]{1,2,0:T(8,128)(2,1)S(1)} %copy-done.3), kind=kOutput, calls=%fused_computation.2 | convolution fusion | flops 470679552 | bytes 5341184 | tf_op jit(solution)/shard_map/dot_general | solution.py:127
  308.5 0.5 all-to-all-done.4
  309.1 0.8 convolution_convert_fusion.4
  (34 shorter events, 2.0 us)
Async XLA Ops:
  7.2 178.0 %copy-start = (bf16[1,112,4096]{2,1,0:T(8,128)(2,1)S(1)}, bf16[1,112,4096]{2,1,0:T(8,128)(2,1)}, u32[]{:S(2)}) copy-start(bf16[1,112,4096]{2,1,0:T(8,128)(2,1)} %param.16) | copy-start | bytes 2752516
  12.1 10.7 %all-to-all-start = ((bf16[4,2,2048]{2,1,0:T(2,128)(2,1)}), bf16[4,2,2048]{2,1,0:T(2,128)(2,1)S(1)}, u32[]{:S(2)}, u32[]{:S(2)}) async-start(bf16[4,2,2048]{2,1,0:T(2,128)(2,1)} %reshape.107), calls=%async_computation | async-start | bytes 65536 | tf_op jit(solution)/shard_map/all_to_all | solution.py:28
  22.9 8.7 %all-to-all-start.5 = ((bf16[4,2,4096]{2,1,0:T(2,128)(2,1)}), bf16[4,2,4096]{2,1,0:T(2,128)(2,1)S(1)}, u32[]{:S(2)}, u32[]{:S(2)}) async-start(bf16[4,2,4096]{2,1,0:T(2,128)(2,1)} %reshape.113), calls=%async_computation.5 | async-start | bytes 131072 | tf_op jit(solution)/shard_map/all_to_all | solution.py:28
  31.6 6.3 %all-to-all-start.1 = ((bf16[2,2,4096]{2,1,0:T(2,128)(2,1)}), bf16[2,2,4096]{2,1,0:T(2,128)(2,1)S(1)}, u32[]{:S(2)}, u32[]{:S(2)}) async-start(bf16[2,2,4096]{2,1,0:T(2,128)(2,1)} %reshape.109), calls=%async_computation.1 | async-start | bytes 65536 | tf_op jit(solution)/shard_map/all_to_all | solution.py:28
  37.9 6.3 %all-to-all-start.6 = ((bf16[2,2,8192]{2,1,0:T(2,128)(2,1)}), bf16[2,2,8192]{2,1,0:T(2,128)(2,1)S(1)}, u32[]{:S(2)}, u32[]{:S(2)}) async-start(bf16[2,2,8192]{2,1,0:T(2,128)(2,1)} %reshape.115), calls=%async_computation.6 | async-start | bytes 131072 | tf_op jit(solution)/shard_map/all_to_all | solution.py:28
  45.8 137.8 %all-to-all-start.2 = ((bf16[64,256,64]{1,2,0:T(8,128)(2,1)}), bf16[64,256,64]{1,2,0:T(8,128)(2,1)S(1)}, u32[]{:S(2)}, u32[]{:S(2)}) async-start(bf16[64,256,64]{1,2,0:T(8,128)(2,1)} %stack.3), calls=%async_computation.2 | async-start | bytes 4194304 | tf_op jit(solution)/shard_map/all_to_all | solution.py:96
  68.6 132.7 %all-gather.3.cloned.1.call-start = ((), (), s32[]{:S(2)}) async-start(), calls=%async_computation.7 | async-start | bytes 2228224 | tf_op jit(solution)/shard_map/all_gather | solution.py:46
  193.5 106.0 %all-to-all-start.3 = ((bf16[64,256,64]{1,2,0:T(8,128)(2,1)}), bf16[64,256,64]{1,2,0:T(8,128)(2,1)S(1)}, u32[]{:S(2)}, u32[]{:S(2)}) async-start(bf16[64,256,64]{1,2,0:T(8,128)(2,1)} %bitcast.126), calls=%async_computation.3 | async-start | bytes 4194304 | tf_op jit(solution)/shard_map/all_to_all | solution.py:39
  201.2 26.7 %all-gather.5.cloned.1.call-start = ((), (), s32[]{:S(2)}) async-start(), calls=%async_computation.8 | async-start | bytes 6291456 | tf_op jit(solution)/shard_map/all_gather | solution.py:46
  227.9 4.7 %copy-start.2 = (bf16[1,512,112]{1,2,0:T(8,128)(2,1)S(1)}, bf16[1,512,112]{1,2,0:T(8,128)(2,1)}, u32[]{:S(2)}) copy-start(bf16[1,512,112]{1,2,0:T(8,128)(2,1)} %param.21) | copy-start | bytes 344068
  227.9 4.7 %copy-start.3 = (bf16[1,512,112]{1,2,0:T(8,128)(2,1)S(1)}, bf16[1,512,112]{1,2,0:T(8,128)(2,1)}, u32[]{:S(2)}) copy-start(bf16[1,512,112]{1,2,0:T(8,128)(2,1)} %param.20) | copy-start | bytes 344068
  230.6 1.9 copy-start.1
  300.7 8.4 %all-to-all-start.4 = ((bf16[8,2,1024]{2,1,0:T(2,128)(2,1)}), bf16[8,2,1024]{2,1,0:T(2,128)(2,1)S(1)}, u32[]{:S(2)}, u32[]{:S(2)}) async-start(bf16[8,2,1024]{2,1,0:T(2,128)(2,1)} %reshape.111), calls=%async_computation.4 | async-start | bytes 65536 | tf_op jit(solution)/shard_map/all_to_all | solution.py:103
Sparse Core Ops, SparseCore 0:
  75.4 114.2 all-gather.2
  204.1 23.7 all-gather.4
